TPU v7x, 32 devices: a whole 2x2x4 slice. The times are simulated.
32 devices in a mesh: ctx: 16 (over z, y, x), head: 2 (over core).
Axes of the slice: x: 2, y: 2, z: 4, core: 2. Of those that a mesh axis runs over, the one named last changes fastest.
Arguments:
- queries: float32 [8192, 512], P('ctx', 'head'), may hold values from -1024 to 1024
- keys: float32 [8192, 128], P('ctx'), may hold values from -1024 to 1024
- values: float32 [8192, 128], P('ctx'), may hold values from -6 to 6
- cotangent: float32 [8192, 512], P('ctx', 'head'), may hold values from -384 to 384
- source_ids: int32 [8192], P('ctx'), may hold values from 0 to 63
- source_weights: float32 [64], replicated, may hold values from 0.25 to 4
- q_feature: float32 [4, 128, 128], P('head'), may hold values from -4 to 4
- k_feature: float32 [128, 128], replicated, may hold values from -4 to 4
Outputs:
- grad_queries: float32 [8192, 512], P('ctx', 'head')
- grad_keys: float32 [8192, 128], P(('ctx', 'head'))
- grad_values: float32 [8192, 128], P(('ctx', 'head'))
- grad_q_feature: float32 [4, 128, 128], P('head')
- grad_k_feature: float32 [128, 128], replicated
All inputs are finite; a program needn't handle non-finite values.
Results may differ from a plain program's by a relative error of at most 0.0015.
Values sent between devices are 32-bit elements; how exact they have to be, the bound alone decides.
No kernel may reach another device: no remote copies, remote signals or barrier semaphores. Data moves between devices by JAX's collectives and lax.ppermute only.
A program may use at most 64 MiB of HBM per device.

v0:
```python
import jax
import jax.numpy as jnp
from jax import lax
from jax.sharding import PartitionSpec as P


def entering(value, axis, join, neutral, backward):
    count, mine = (lax.axis_size(axis), lax.axis_index(axis))
    pieces = jax.tree.map(lambda part: lax.all_gather(part, axis), value)
    if backward:
        pieces = jax.tree.map(lambda part: part[::-1], pieces)
        mine = count - 1 - mine
    total = jax.tree.map(
        lambda part, zero: jnp.full_like(part, 0) + jnp.asarray(zero, part.dtype), value, neutral
    )

    def turn(position, total):
        longer = join(total, jax.tree.map(lambda part: part[position], pieces))
        return jax.tree.map(lambda new, old: jnp.where(position < mine, new, old), longer, total)

    return lax.fori_loop(0, count - 1, turn, total)


def matmul(left, right):
    return jnp.dot(left, right, precision=lax.Precision.HIGHEST, preferred_element_type=jnp.float32)


def product(form, left, right):
    return jnp.einsum(
        form, left, right, precision=lax.Precision.HIGHEST, preferred_element_type=jnp.float32
    )


def feature_map(inputs, weight):
    logits = matmul(inputs, weight)
    upper = jax.nn.softmax(logits, axis=-1)
    lower = jax.nn.softmax(-logits, axis=-1)
    return (jnp.concatenate([upper, lower], axis=-1), upper, lower)


def feature_back(inputs, weight, upper, lower, grad_feat):
    half = upper.shape[-1]
    grad_upper = grad_feat[:, :half]
    grad_lower = grad_feat[:, half:]
    grad_logits = upper * (grad_upper - jnp.sum(upper * grad_upper, axis=-1, keepdims=True))
    grad_logits = grad_logits - lower * (
        grad_lower - jnp.sum(lower * grad_lower, axis=-1, keepdims=True)
    )
    return (matmul(grad_logits, weight.T), matmul(inputs.T, grad_logits))


def causal_mask(count):
    row_index = lax.broadcasted_iota(jnp.int32, (count, count), 0)
    col_index = lax.broadcasted_iota(jnp.int32, (count, count), 1)
    return (row_index >= col_index).astype(jnp.float32)


def add_pair(earlier, later):
    return (earlier[0] + later[0], earlier[1] + later[1])


def block_terms(query_c, key_c, value_c, scaled_c, prefix, prefix_tot):
    lower_mask = causal_mask(query_c.shape[1])
    scores = product("ncf,ndf->ncd", query_c, key_c) * lower_mask
    numerator = product("ncd,nde->nce", scores, value_c) + product("ncf,nfe->nce", query_c, prefix)
    normalizer = jnp.sum(scores, axis=2) + product("ncf,nf->nc", query_c, prefix_tot)
    output = numerator / normalizer[..., None]
    grad_numer = scaled_c / normalizer[..., None]
    grad_norm = -jnp.sum(scaled_c * output, axis=2) / normalizer
    grad_scores = (product("nce,nde->ncd", grad_numer, value_c) + grad_norm[..., None]) * lower_mask
    grad_query = (
        product("ncd,ndf->ncf", grad_scores, key_c)
        + product("nce,nfe->ncf", grad_numer, prefix)
        + grad_norm[..., None] * prefix_tot[:, None, :]
    )
    grad_key = product("ncd,ncf->ndf", grad_scores, query_c)
    grad_value = product("ncd,nce->nde", scores, grad_numer)
    carried = product("ncf,nce->nfe", query_c, grad_numer)
    carried_totals = product("nc,ncf->nf", grad_norm, query_c)
    return (grad_query, grad_key, grad_value, carried, carried_totals)


def on_device(queries, keys, values, cotangent, source_ids, source_weights, q_feature, k_feature):
    head_count = q_feature.shape[0]
    width = q_feature.shape[1]
    features = 2 * q_feature.shape[2]
    rows = queries.shape[0]
    piece = min(128, rows)
    pieces = rows // piece
    source_index = lax.broadcasted_iota(jnp.int32, (1, source_weights.shape[0]), 1)
    lookup = (source_ids[:, None] == source_index).astype(jnp.float32)
    weight = jnp.sum(lookup * source_weights[None, :], axis=1)
    key_feat, key_upper, key_lower = feature_map(keys, k_feature)
    key_c = key_feat.reshape(pieces, piece, features)
    value_c = values.reshape(pieces, piece, width)
    piece_state = product("ncf,nce->nfe", key_c, value_c)
    piece_tot = jnp.sum(key_c, axis=1)
    share = features // lax.axis_size("head")
    offset = lax.axis_index("head") * share
    slab_feat = lax.dynamic_slice_in_dim(key_feat, offset, share, 1)
    slab_local = (
        lax.dynamic_slice_in_dim(jnp.sum(piece_state, axis=0), offset, share, 0),
        lax.dynamic_slice_in_dim(jnp.sum(piece_tot, axis=0), offset, share, 0),
    )
    slab_zero = (jnp.zeros((share, width), jnp.float32), jnp.zeros((share,), jnp.float32))
    slab_before = entering(slab_local, "ctx", add_pair, slab_zero, False)
    earlier, earlier_totals = (
        lax.all_gather(slab_before[0], "head", axis=0, tiled=True),
        lax.all_gather(slab_before[1], "head", axis=0, tiled=True),
    )
    prefix = jnp.cumsum(piece_state, axis=0) - piece_state + earlier[None]
    prefix_tot = jnp.cumsum(piece_tot, axis=0) - piece_tot + earlier_totals[None]
    grad_keyfeat = jnp.zeros(key_feat.shape, jnp.float32)
    grad_vals = jnp.zeros(values.shape, jnp.float32)
    piece_carried = jnp.zeros((pieces, features, width), jnp.float32)
    piece_carried_tot = jnp.zeros((pieces, features), jnp.float32)
    query_grads = []
    weight_grads = []
    for head in range(head_count):
        query_head = queries[:, head * width : (head + 1) * width]
        query_feat, query_upper, query_lower = feature_map(query_head, q_feature[head])
        scaled = cotangent[:, head * width : (head + 1) * width] * weight[:, None]
        grad_query, grad_key, grad_value, carried, carried_totals = block_terms(
            query_feat.reshape(pieces, piece, features),
            key_c,
            value_c,
            scaled.reshape(pieces, piece, width),
            prefix,
            prefix_tot,
        )
        grad_head, grad_weight = feature_back(
            query_head,
            q_feature[head],
            query_upper,
            query_lower,
            grad_query.reshape(rows, features),
        )
        query_grads.append(grad_head)
        weight_grads.append(grad_weight)
        grad_keyfeat = grad_keyfeat + grad_key.reshape(rows, features)
        grad_vals = grad_vals + grad_value.reshape(rows, width)
        piece_carried = piece_carried + carried
        piece_carried_tot = piece_carried_tot + carried_totals
    carried_all = jnp.sum(piece_carried, axis=0)
    carried_tot = jnp.sum(piece_carried_tot, axis=0)
    inner_later = carried_all[None] - jnp.cumsum(piece_carried, axis=0)
    inner_tot = carried_tot[None] - jnp.cumsum(piece_carried_tot, axis=0)
    grad_keyfeat = grad_keyfeat + (
        product("nce,nfe->ncf", value_c, inner_later) + inner_tot[:, None, :]
    ).reshape(rows, features)
    grad_vals = grad_vals + product("ncf,nfe->nce", key_c, inner_later).reshape(rows, width)
    folded, folded_tot = (
        lax.psum_scatter(carried_all, "head", scatter_dimension=0, tiled=True),
        lax.psum_scatter(carried_tot, "head", scatter_dimension=0, tiled=True),
    )
    later, later_tot = entering((folded, folded_tot), "ctx", add_pair, slab_zero, True)
    slab_grad = matmul(values, later.T) + later_tot[None, :]
    current = lax.dynamic_slice_in_dim(grad_keyfeat, offset, share, 1)
    grad_keyfeat = lax.dynamic_update_slice_in_dim(grad_keyfeat, current + slab_grad, offset, 1)
    grad_vals = grad_vals + matmul(slab_feat, later)
    grad_key_part, grad_kweight = feature_back(keys, k_feature, key_upper, key_lower, grad_keyfeat)
    grad_keys, grad_values = (
        lax.psum_scatter(grad_key_part, "head", scatter_dimension=0, tiled=True),
        lax.psum_scatter(grad_vals, "head", scatter_dimension=0, tiled=True),
    )
    grad_qweight = lax.psum(jnp.stack(weight_grads, axis=0), "ctx")
    grad_kweight = lax.psum(grad_kweight, ("ctx", "head"))
    return (
        jnp.concatenate(query_grads, axis=1),
        grad_keys,
        grad_values,
        grad_qweight,
        grad_kweight,
    )


def solution(mesh):
    placed = (
        P("ctx", "head"),
        P("ctx", None),
        P("ctx", None),
        P("ctx", "head"),
        P("ctx"),
        P(),
        P("head", None, None),
        P(),
    )
    return jax.shard_map(
        on_device,
        mesh=mesh,
        in_specs=placed,
        out_specs=(
            P("ctx", "head"),
            P(("ctx", "head"), None),
            P(("ctx", "head"), None),
            P("head", None, None),
            P(),
        ),
        check_vma=False,
    )
```

profile of v0, /device:TPU:0, one launch (start us, length us, event | category | flops | bytes accessed | tf_op | source)
XLA Modules:
  0.0 441.5 jit_solution(6858536777643410984)
XLA Ops:
  7.2 1.4 fusion.102
  16.1 42.4 %all-gather.4 = f32[16,1,128]{2,1,0:T(1,128)S(1)} all-gather(f32[1,1,128]{2,1,0:T(1,128)S(1)} %dynamic-slice_bitcast_fusion.1), channel_id=3, replica_groups=mesh['ctx'=16,'head'=2] {'ctx'}, dimensions={0}, use_global_device_ids=true | all-gather | bytes 8704 | tf_op jit(solution)/shard_map/all_gather | solution.py:9
  59.9 1.8 fusion.107
  61.7 1.8 fusion.109
  63.4 5.7 %all-gather.10.cloned.1.call-done = f32[2048,128]{1,0:T(8,128)} async-done(((f32[128,128]{1,0:T(8,128)}), f32[2048,128]{1,0:T(8,128)}) %all-gather.10.cloned.1.call-update) | async-done | bytes 1048592 | tf_op jit(solution)/shard_map/all_gather | solution.py:9
  69.2 13.6 %while.32 = (s32[]{:T(128)}, f32[128,128]{1,0:T(8,128)S(1)}, f32[128]{0:T(128)S(1)}, s32[]{:T(128)}, f32[16,128,128]{2,1,0:T(8,128)}, /*index=5*/f32[16,128]{1,0:T(8,128)S(1)}, s32[]{:T(128)}, s32[]{:T(128)}) while((s32[]{:T(128)}, f32[128,128]{1,0:T(8,128)S(1)}, f32[128]{0:T(128)S(1)}, s32[]{:T(128)}, ...), condition=%wide.region_15.16_spmd.clone, body=%wide.region_14.15_spmd.clone.sunk | while | flops 49540 | bytes 198267 | solution.py:21
  82.8 1.8 all-gather.5
  86.8 2.1 all_gather.35
  93.0 1.4 fusion.45
  94.4 1.4 fusion.33
  95.9 1.4 fusion.36
  100.2 2.5 all-reduce
  103.7 1.4 convolution_add_fusion.2
  108.9 2.1 fusion.110
  111.1 1.2 reduce-window_subtract_fusion
  112.3 1.4 fusion.2
  113.7 3.9 reduce-scatter.4.cloned.1.call-done
  117.8 41.0 %all-gather.6 = f32[16,1,128]{2,1,0:T(1,128)S(1)} all-gather(f32[1,1,128]{2,1,0:T(1,128)S(1)} %dynamic-slice_bitcast_fusion), channel_id=5, replica_groups=mesh['ctx'=16,'head'=2] {'ctx'}, dimensions={0}, use_global_device_ids=true | all-gather | bytes 8704 | tf_op jit(solution)/shard_map/all_gather | solution.py:9
  158.8 1.8 copy.212
  162.5 1.2 copy.209
  163.7 1.8 copy.211
  165.5 1.2 multiply_reduce_fusion.2
  173.0 3.7 all-gather.12.cloned.1.call-done
  176.7 1.3 rev.6
  181.6 1.3 convolution_add_fusion.5
  183.7 1.3 fusion.111
  187.8 99.0 %all-reduce.4.cloned.1.call-done = f32[2,128,128]{1,2,0:T(8,128)} async-done(((f32[2,128,128]{1,2,0:T(8,128)}), f32[2,128,128]{1,2,0:T(8,128)}) %all-reduce.4.cloned.1.call-update) | async-done | bytes 131088 | tf_op jit(solution)/shard_map/psum | solution.py:166
  286.8 1.7 copy.181
  288.4 122.9 %all-reduce.6.cloned.1.call-done = f32[128,128]{0,1:T(8,128)} async-done(((f32[128,128]{0,1:T(8,128)}), f32[128,128]{0,1:T(8,128)}) %all-reduce.6.cloned.1.call-update) | async-done | bytes 65552 | tf_op jit(solution)/shard_map/psum | solution.py:167
  411.3 1.6 copy.182
  412.8 10.1 %reduce-scatter.8.cloned.1.call-done = f32[256,128]{1,0:T(8,128)} async-done(((f32[512,128]{1,0:T(8,128)}), f32[256,128]{1,0:T(8,128)}) %reduce-scatter.8.cloned.1.call-update) | async-done | bytes 131088 | tf_op jit(solution)/shard_map/reduce_scatter | solution.py:164
  422.9 11.7 %reduce-scatter.6.cloned.1.call-done = f32[256,128]{1,0:T(8,128)} async-done(((f32[512,128]{1,0:T(8,128)}), f32[256,128]{1,0:T(8,128)}) %reduce-scatter.6.cloned.1.call-update) | async-done | bytes 131088 | tf_op jit(solution)/shard_map/reduce_scatter | solution.py:163
  (229 shorter events, 51.1 us)
Async XLA Ops:
  7.2 1.8 copy-start
  7.2 62.0 %all-gather.10.cloned.1.call-start = ((), (), s32[]{:S(2)}) async-start(), calls=%async_computation.8 | async-start | bytes 1114112 | tf_op jit(solution)/shard_map/all_gather | solution.py:9
  9.0 2.0 copy-start.29
  10.3 107.3 %reduce-scatter.4.cloned.1.call-start = ((), (), s32[]{:S(2)}) async-start(), calls=%async_computation.3 | async-start | bytes 196608 | tf_op jit(solution)/shard_map/reduce_scatter | solution.py:153
  13.1 45.4 %copy-start.12 = (f32[512,256]{1,0:T(8,128)S(1)}, f32[512,256]{1,0:T(8,128)}, u32[]{:S(2)}) copy-start(f32[512,256]{1,0:T(8,128)} %param.12) | copy-start | bytes 1572868
  13.5 45.1 %copy-start.27 = (f32[2,128,128]{2,1,0:T(8,128)S(1)}, f32[2,128,128]{2,1,0:T(8,128)}, u32[]{:S(2)}) copy-start(f32[2,128,128]{2,1,0:T(8,128)} %param.18) | copy-start | bytes 393220
  58.6 3.1 copy-start.24
  69.2 15.4 %copy-start.15 = (f32[4,256]{0,1:T(8,128)S(1)}, f32[4,256]{0,1:T(8,128)}, u32[]{:S(2)}) copy-start(f32[4,256]{0,1:T(8,128)} %copy-done.14) | copy-start | bytes 12292
  90.0 1.8 copy-start.16
  90.0 1.8 copy-start.31
  91.8 4.1 copy-start.33
  95.9 2.1 copy-start.1
  95.9 2.1 copy-start.20
  105.7 1.2 copy-start.10
  105.7 1.3 copy-start.17
  105.7 1.3 copy-start.34
  107.7 1.2 copy-start.26
  111.0 65.7 %all-gather.12.cloned.1.call-start = ((), (), s32[]{:S(2)}) async-start(), calls=%async_computation.9 | async-start | bytes 1114112 | tf_op jit(solution)/shard_map/all_gather | solution.py:9
  111.1 1.2 copy-start.9
  117.6 169.1 %all-reduce.4.cloned.1.call-start = ((), (), s32[]{:S(2)}) async-start(), calls=%async_computation.6 | async-start | bytes 262144 | tf_op jit(solution)/shard_map/psum | solution.py:166
  158.8 1.9 copy-start.22
  165.5 1.2 copy-start.7
  165.5 1.2 copy-start.8
  167.7 1.1 copy-start.6
  169.1 1.1 copy-start.32
  171.2 1.1 copy-start.2
  171.2 1.1 copy-start.21
  173.0 238.3 %all-reduce.6.cloned.1.call-start = ((), (), s32[]{:S(2)}) async-start(), calls=%async_computation.7 | async-start | bytes 131072 | tf_op jit(solution)/shard_map/psum | solution.py:167
  176.7 1.3 copy-start.35
  181.5 241.4 %reduce-scatter.8.cloned.1.call-start = ((), (), s32[]{:S(2)}) async-start(), calls=%async_computation.5 | async-start | bytes 393216 | tf_op jit(solution)/shard_map/reduce_scatter | solution.py:164
  182.9 251.7 %reduce-scatter.6.cloned.1.call-start = ((), (), s32[]{:S(2)}) async-start(), calls=%async_computation.4 | async-start | bytes 393216 | tf_op jit(solution)/shard_map/reduce_scatter | solution.py:163
  183.7 1.3 copy-start.28
  (16 other events, 13.4 us)
Sparse Core Ops, SparseCore 0:
  11.3 57.8 all-gather.9
  111.1 6.4 reduce-scatter.3
  120.4 56.2 all-gather.11
  182.6 104.1 all-reduce.3
  292.8 118.4 all-reduce.5
  413.9 8.9 reduce-scatter.7
  425.7 8.8 reduce-scatter.5
where the time goes:
time: 443 us; the launch traced here: 441 us
  waiting for transfers between devices  257 us (58%)
  blocking collectives  89.8 us (20%)
  matrix products  32.6 us (7%)
  local copies, waits for them, and re-layouts  26.5 us (6%)
  other arithmetic  19 us (4%)
  between operations  15.4 us (3%)
    psum x1, waiting for transfers between devices, on_device(): grad_kweight = lax.psum(grad_kweight, ('ctx', 'head'))  123 us
    psum x1, waiting for transfers between devices, on_device(): grad_qweight = lax.psum(jnp.stack(weight_grads, axis=0), 'ctx')  99 us
    all_gather x2, blocking collectives, entering(): pieces = jax.tree.map(lambda part: lax.all_gather(part, axis), value)  83.5 us
    dot_general x25, matrix products, product(): jnp.einsum(form, left, right, precision=lax.Precision.HIGHEST, preferred_...  24.8 us
    unnamed x92, local copies, waits for them, and re-layouts  19.6 us
    select_n x60, other arithmetic, turn(): jnp.where(position < mine, new, old)  13.7 us
    reduce_scatter x1, waiting for transfers between devices, on_device(): lax.psum_scatter(grad_key_part, 'head', scatter_dimension=0, tiled=True)  11.7 us
    reduce_scatter x1, waiting for transfers between devices, on_device(): lax.psum_scatter(grad_vals, 'head', scatter_dimension=0, tiled=True)  10.1 us
  transfers between devices with their start and end apart: 7, of which 7 were waited for; matrix products, arithmetic and copies ran while one was open for 8% of the time, Pallas kernels for 0%

commit v1 on v0

--- a/solution.py
+++ b/solution.py
@@ -164,7 +164,7 @@
         lax.psum_scatter(grad_vals, "head", scatter_dimension=0, tiled=True),
     )
     grad_qweight = lax.psum(jnp.stack(weight_grads, axis=0), "ctx")
-    grad_kweight = lax.psum(grad_kweight, ("ctx", "head"))
+    grad_kweight = lax.psum(lax.psum(grad_kweight, "head"), "ctx")
     return (
         jnp.concatenate(query_grads, axis=1),
         grad_keys,

time: 443 us -> 406 us (0.916)
  waiting for transfers between devices: 257 us -> 196 us
  other arithmetic: 19 us -> 41.9 us
    psum x1, waiting for transfers between devices: 123 us -> 16 us  [on_device(): grad_kweight = lax.psum(lax.psum(grad_kweight, 'head'), 'ctx')]
    all_gather x2, waiting for transfers between devices: 9.41 us -> 52.2 us  [entering(): pieces = jax.tree.map(lambda part: lax.all_gather(part, axis), value)]
    select_n x60, other arithmetic: 13.7 us -> 36.6 us  [turn(): jnp.where(position < mine, new, old)]
    psum x1, waiting for transfers between devices: 99 us -> 109 us  [on_device(): grad_qweight = lax.psum(jnp.stack(weight_grads, axis=0), 'ctx')]
    unnamed x92 -> x80, local copies, waits for them, and re-layouts: 19.6 us -> 17.5 us
  transfers between devices with their start and end apart: 7 -> 7, of which waited for: 7 -> 7; matrix products, arithmetic and copies ran while one was open for 8% -> 7% of each run, Pallas kernels for 0% -> 0%
where the time goes in v1:
time: 406 us; the launch traced here: 404 us
  waiting for transfers between devices  196 us (48%)
  blocking collectives  87.3 us (22%)
  other arithmetic  41.9 us (10%)
  matrix products  34.6 us (9%)
  local copies, waits for them, and re-layouts  26.9 us (7%)
  between operations  15.3 us (4%)
    psum x1, waiting for transfers between devices, on_device(): grad_qweight = lax.psum(jnp.stack(weight_grads, axis=0), 'ctx')  109 us
    all_gather x2, blocking collectives, entering(): pieces = jax.tree.map(lambda part: lax.all_gather(part, axis), value)  80.9 us
    all_gather x2, waiting for transfers between devices, entering(): pieces = jax.tree.map(lambda part: lax.all_gather(part, axis), value)  52.2 us
    select_n x60, other arithmetic, turn(): jnp.where(position < mine, new, old)  36.6 us
    dot_general x25, matrix products, product(): jnp.einsum(form, left, right, precision=lax.Precision.HIGHEST, preferred_...  26.7 us
    unnamed x80, local copies, waits for them, and re-layouts  17.5 us
    psum x1, waiting for transfers between devices, on_device(): grad_kweight = lax.psum(lax.psum(grad_kweight, 'head'), 'ctx')  16 us
    reduce_scatter x1, waiting for transfers between devices, on_device(): lax.psum_scatter(grad_key_part, 'head', scatter_dimension=0, tiled=True)  11.7 us
  transfers between devices with their start and end apart: 7, of which 7 were waited for; matrix products, arithmetic and copies ran while one was open for 7% of the time, Pallas kernels for 0%

profile of v1, /device:TPU:0, one launch (start us, length us, event | category | flops | bytes accessed | tf_op | source)
XLA Modules:
  0.0 403.6 jit_solution(6624324895267392985)
XLA Ops:
  7.2 1.4 fusion.102
  15.7 42.4 %all-gather.4 = f32[16,1,128]{2,1,0:T(1,128)S(1)} all-gather(f32[1,1,128]{2,1,0:T(1,128)S(1)} %dynamic-slice_bitcast_fusion.1), channel_id=3, replica_groups=mesh['ctx'=16,'head'=2] {'ctx'}, dimensions={0}, use_global_device_ids=true | all-gather | bytes 8704 | tf_op jit(solution)/shard_map/all_gather | solution.py:9
  59.4 1.8 fusion.107
  61.2 1.8 fusion.109
  63.0 6.2 %all-gather.10.cloned.1.call-done = f32[2048,128]{1,0:T(8,128)} async-done(((f32[128,128]{1,0:T(8,128)}), f32[2048,128]{1,0:T(8,128)}) %all-gather.10.cloned.1.call-update) | async-done | bytes 1048592 | tf_op jit(solution)/shard_map/all_gather | solution.py:9
  69.2 13.6 %while.32 = (s32[]{:T(128)}, f32[128,128]{1,0:T(8,128)S(1)}, f32[128]{0:T(128)S(1)}, s32[]{:T(128)}, f32[16,128,128]{2,1,0:T(8,128)}, /*index=5*/f32[16,128]{1,0:T(8,128)S(1)}, s32[]{:T(128)}, s32[]{:T(128)}) while((s32[]{:T(128)}, f32[128,128]{1,0:T(8,128)S(1)}, f32[128]{0:T(128)S(1)}, s32[]{:T(128)}, ...), condition=%wide.region_15.16_spmd.clone, body=%wide.region_14.15_spmd.clone.sunk | while | flops 49540 | bytes 198267 | solution.py:21
  82.8 1.8 all-gather.5
  86.8 2.1 all_gather.35
  92.8 1.4 fusion.45
  94.2 1.4 fusion.33
  95.6 1.4 fusion.36
  99.9 2.5 all-reduce
  102.4 38.5 %all-gather.6 = f32[16,1,128]{2,1,0:T(1,128)S(1)} all-gather(f32[1,1,128]{2,1,0:T(1,128)S(1)} %dynamic-slice_bitcast_fusion), channel_id=5, replica_groups=mesh['ctx'=16,'head'=2] {'ctx'}, dimensions={0}, use_global_device_ids=true | all-gather | bytes 8704 | tf_op jit(solution)/shard_map/all_gather | solution.py:9
  142.6 1.4 convolution_add_fusion.2
  146.3 1.8 copy.213
  148.1 2.6 fusion.4
  150.7 2.1 fusion.110
  152.9 1.2 reduce-window_subtract_fusion
  154.1 1.4 fusion.2
  156.7 1.8 fusion.105
  159.3 1.2 copy.209
  160.6 1.8 copy.211
  169.4 46.0 %all-gather.12.cloned.1.call-done = f32[2048,128]{1,0:T(8,128)} async-done(((f32[128,128]{1,0:T(8,128)}), f32[2048,128]{1,0:T(8,128)}) %all-gather.12.cloned.1.call-update) | async-done | bytes 1048592 | tf_op jit(solution)/shard_map/all_gather | solution.py:9
  215.4 2.4 rev.6
  217.8 23.7 %while.33 = (s32[]{:T(128)}, f32[128,128]{1,0:T(8,128)S(1)}, f32[128]{0:T(128)S(1)}, s32[]{:T(128)}, f32[16,128,128]{2,1,0:T(8,128)}, /*index=5*/f32[16,128]{1,0:T(8,128)}, s32[]{:T(128)}, s32[]{:T(128)}) while((s32[]{:T(128)}, f32[128,128]{1,0:T(8,128)S(1)}, f32[128]{0:T(128)S(1)}, s32[]{:T(128)}, f32[16,128,128]{2,1,0:T(8,128)}, ...), condition=%wide.region_35.36_spmd.clone, body=%wide.region_34.35_spmd.clone.sunk | while | flops 49540 | bytes 198267 | solution.py:21
  244.7 16.0 %all-reduce.5.cloned.1.call-done = f32[128,128]{0,1:T(8,128)} async-done(((f32[128,128]{0,1:T(8,128)}), f32[128,128]{0,1:T(8,128)}) %all-reduce.5.cloned.1.call-update) | async-done | bytes 65552 | tf_op jit(solution)/shard_map/psum | solution.py:167
  260.8 1.3 convolution_add_fusion.5
  262.9 1.3 fusion.111
  267.0 108.6 %all-reduce.7.cloned.1.call-done = (f32[2,128,128]{1,2,0:T(8,128)}, f32[128,128]{0,1:T(8,128)}) async-done(((f32[2,128,128]{1,2,0:T(8,128)}, f32[128,128]{0,1:T(8,128)}), (f32[2,128,128]{1,2,0:T(8,128)}, f32[128,128]{0,1:T(8,128)})) %all-reduce.7.cloned.1.call-update) | async-done | bytes 196624 | tf_op jit(solution)/shard_map/psum | solution.py:166
  375.6 1.7 copy.181
  378.0 7.0 %reduce-scatter.8.cloned.1.call-done = f32[256,128]{1,0:T(8,128)} async-done(((f32[512,128]{1,0:T(8,128)}), f32[256,128]{1,0:T(8,128)}) %reduce-scatter.8.cloned.1.call-update) | async-done | bytes 131088 | tf_op jit(solution)/shard_map/reduce_scatter | solution.py:164
  385.1 11.7 %reduce-scatter.6.cloned.1.call-done = f32[256,128]{1,0:T(8,128)} async-done(((f32[512,128]{1,0:T(8,128)}), f32[256,128]{1,0:T(8,128)}) %reduce-scatter.6.cloned.1.call-update) | async-done | bytes 131088 | tf_op jit(solution)/shard_map/reduce_scatter | solution.py:163
  (217 shorter events, 73.7 us)
Async XLA Ops:
  7.2 1.8 copy-start
  7.2 62.0 %all-gather.10.cloned.1.call-start = ((), (), s32[]{:S(2)}) async-start(), calls=%async_computation.7 | async-start | bytes 1114112 | tf_op jit(solution)/shard_map/all_gather | solution.py:9
  9.0 2.0 copy-start.22
  10.3 146.1 %reduce-scatter.4.cloned.1.call-start = ((), (), s32[]{:S(2)}) async-start(), calls=%async_computation.3 | async-start | bytes 196608 | tf_op jit(solution)/shard_map/reduce_scatter | solution.py:153
  13.1 45.0 %copy-start.11 = (f32[512,256]{1,0:T(8,128)S(1)}, f32[512,256]{1,0:T(8,128)}, u32[]{:S(2)}) copy-start(f32[512,256]{1,0:T(8,128)} %param.12) | copy-start | bytes 1572868
  13.5 44.6 %copy-start.20 = (f32[2,128,128]{2,1,0:T(8,128)S(1)}, f32[2,128,128]{2,1,0:T(8,128)}, u32[]{:S(2)}) copy-start(f32[2,128,128]{2,1,0:T(8,128)} %param.18) | copy-start | bytes 393220
  90.0 1.8 copy-start.13
  90.0 1.8 copy-start.24
  91.7 3.9 copy-start.27
  95.6 2.1 copy-start.1
  95.6 2.1 copy-start.17
  141.6 1.0 copy-start.10
  146.3 1.8 copy-start.14
  146.3 1.8 copy-start.28
  148.1 2.6 copy-start.19
  152.8 62.6 %all-gather.12.cloned.1.call-start = ((), (), s32[]{:S(2)}) async-start(), calls=%async_computation.8 | async-start | bytes 1114112 | tf_op jit(solution)/shard_map/all_gather | solution.py:9
  152.8 1.2 copy-start.9
  156.4 104.3 %all-reduce.5.cloned.1.call-start = ((), (), s32[]{:S(2)}) async-start(), calls=%async_computation.6 | async-start | bytes 131072 | tf_op jit(solution)/shard_map/psum | solution.py:167
  162.4 1.2 copy-start.5
  162.4 1.2 copy-start.6
  163.6 1.0 copy-start.12
  164.6 1.0 copy-start.7
  164.6 1.1 copy-start.8
  166.0 1.0 copy-start.25
  167.7 1.1 copy-start.2
  167.7 1.1 copy-start.18
  215.4 2.4 copy-start.29
  244.0 131.6 %all-reduce.7.cloned.1.call-start = ((), (), s32[]{:S(2)}) async-start(), calls=%async_computation.9 | async-start | bytes 393216 | tf_op jit(solution)/shard_map/psum | solution.py:166
  260.7 124.3 %reduce-scatter.8.cloned.1.call-start = ((), (), s32[]{:S(2)}) async-start(), calls=%async_computation.5 | async-start | bytes 393216 | tf_op jit(solution)/shard_map/reduce_scatter | solution.py:164
  262.1 134.6 %reduce-scatter.6.cloned.1.call-start = ((), (), s32[]{:S(2)}) async-start(), calls=%async_computation.4 | async-start | bytes 393216 | tf_op jit(solution)/shard_map/reduce_scatter | solution.py:163
  262.9 1.3 copy-start.21
  375.6 1.7 copy-start.26
  (10 other events, 7.8 us)
Sparse Core Ops, SparseCore 0:
  11.3 57.8 all-gather.9
  152.9 3.4 reduce-scatter.3
  159.2 56.1 all-gather.11
  244.1 16.5 all-reduce.4
  266.4 109.1 all-reduce.6
  378.3 6.7 reduce-scatter.7
  387.9 8.8 reduce-scatter.5
